TPU v7x, 256 devices: a whole 4x4x8 slice. The times are simulated.
256 devices in a mesh: lon: 32 (over z, x_lo, core), lat: 8 (over y, x_hi).
Axes of the slice: x: 4 (x_hi: 2, x_lo: 2; x = x_hi * 2 + x_lo), y: 4, z: 8, core: 2. Of those that a mesh axis runs over, the one named last changes fastest.
Arguments:
- field: bfloat16 [2, 256, 768, 128], P(None, 'lat', 'lon'), may hold values from -6 to 6
- cotangent: bfloat16 [2, 256, 768, 128], P(None, 'lat', 'lon'), may hold values from -6 to 6
- first_weights: bfloat16 [3, 3, 128, 128], replicated, may hold values from -0.1875 to 0.1875
- second_weights: bfloat16 [3, 3, 128, 128], replicated, may hold values from -0.1875 to 0.1875
Outputs:
- output: bfloat16 [2, 256, 768, 128], P(None, 'lat', 'lon')
- field_grad: bfloat16 [2, 256, 768, 128], P(None, 'lat', 'lon')
- first_grad: float32 [3, 3, 128, 128], replicated
- second_grad: float32 [3, 3, 128, 128], replicated
All inputs are finite; a program needn't handle non-finite values.
Results may differ from a plain program's by a relative error of at most 0.0032.
Values may be sent and summed in bfloat16 or wider, within the bound.
A program may use at most 64 MiB of HBM per device.

v0:
```python
import jax
import jax.numpy as jnp
from jax import lax
from jax.experimental import pallas as pl
from jax.experimental.pallas import tpu as pltpu
from jax.sharding import PartitionSpec as P

HALF = 576
PIECE = 40
WIDE = 384
PAIRS, COLS = 16, 24
F32, BF16 = jnp.float32, jnp.bfloat16
SIDES = [(v, h) for v in (-1, 0, 1) for h in (-1, 0, 1) if (v, h) != (0, 0)]


def positions():
    lon = lax.axis_index("lon")
    lat = lax.axis_index("lat")
    core = lon % 2
    x_lo = (lon // 2) % 2
    depth = lon // 4
    return lon, lat, core, x_lo, depth


def offset_of(piece):
    return pl.multiple_of(((9 * piece) // 2) * 8, 8)


class Sum:
    def __init__(self, partial, final, half, pair, plane, column, gathered, sems):
        self.partial, self.final = partial, final
        self.half, self.pair, self.plane, self.column, self.gathered = half, pair, plane, column, gathered
        self.pair_sem, self.plane_sem, self.column_sem, self.gather_sem, self.share_sem = sems
        self.lon, self.lat, self.core, self.x_lo, self.depth = positions()
        self.member = self.x_lo * 8 + self.lat

    def plane_peer(self, step):
        peer = (self.member + step) % 16
        return peer, {"lon": self.depth * 4 + (peer // 8) * 2 + self.core, "lat": peer % 8}

    def column_peer(self, step):
        peer = (self.depth + step) % 8
        return peer, {"lon": peer * 4 + self.x_lo * 2 + self.core, "lat": self.lat}

    def partner(self):
        return {"lon": self.lon + 1 - 2 * self.core, "lat": self.lat}

    def remote(self, src, dst, send, recv, device):
        return pltpu.make_async_remote_copy(
            src_ref=src, dst_ref=dst, send_sem=send, recv_sem=recv,
            device_id=device, device_id_type=pl.DeviceIdType.MESH,
        )

    def pair_copy(self):
        other = pl.multiple_of((1 - self.core) * HALF, 8)
        return self.remote(
            self.partial.at[pl.ds(other, HALF)], self.pair, self.pair_sem.at[0], self.pair_sem.at[1], self.partner()
        )

    def plane_copy(self, step, receiving=False):
        peer, device = self.plane_peer(step)
        slot = peer if receiving else self.member
        return self.remote(
            self.half.at[pl.ds(offset_of(peer), PIECE)], self.plane.at[slot],
            self.plane_sem.at[0, peer], self.plane_sem.at[1, slot], device,
        )

    def column_copy(self, step, receiving=False):
        peer, device = self.column_peer(step)
        slot = peer if receiving else self.depth
        return self.remote(
            self.column.at[self.depth], self.column.at[slot],
            self.column_sem.at[0, peer], self.column_sem.at[1, slot], device,
        )

    def gather_copy(self, step, receiving=False):
        peer, device = self.plane_peer(step)
        slot = peer if receiving else self.member
        return self.remote(
            self.gathered.at[self.core, self.member], self.gathered.at[self.core, slot],
            self.gather_sem.at[0, peer], self.gather_sem.at[1, slot], device,
        )

    def share_copy(self, half):
        return self.remote(
            self.gathered.at[half], self.gathered.at[half], self.share_sem.at[0], self.share_sem.at[1], self.partner()
        )

    def each(self, count, act):
        def step(index, carry):
            act(index)
            return carry

        lax.fori_loop(1, count, step, 0)

    def start(self):
        self.pair_copy().start()

    def to_plane(self):
        self.pair_copy().wait_recv()
        own = pl.multiple_of(self.core * HALF, 8)
        self.half[...] = self.partial[pl.ds(own, HALF)] + self.pair[...]
        self.each(16, lambda step: self.plane_copy(step).start())
        self.plane[self.member] = self.half[pl.ds(offset_of(self.member), PIECE)]

    def to_column(self):
        self.each(16, lambda step: self.plane_copy(step, True).wait_recv())
        total = self.plane[0]
        for member in range(1, 16):
            total = total + self.plane[member]
        self.column[self.depth] = total
        self.each(8, lambda step: self.column_copy(step).start())

    def to_gather(self):
        self.each(8, lambda step: self.column_copy(step, True).wait_recv())
        total = self.column[0]
        for plane in range(1, 8):
            total = total + self.column[plane]
        self.gathered[self.core, self.member] = total.astype(jnp.bfloat16)
        self.each(16, lambda step: self.gather_copy(step).start())

    def to_share(self):
        self.each(16, lambda step: self.gather_copy(step, True).wait_recv())
        self.share_copy(self.core).start()

    def finish(self):
        self.share_copy(1 - self.core).wait_recv()
        for half in range(2):
            for piece in range(16):
                first = half * HALF + ((9 * piece) // 2) * 8
                self.final[pl.ds(first, PIECE)] = self.gathered[half, piece]
        self.pair_copy().wait_send()
        self.each(16, lambda step: self.plane_copy(step).wait_send())
        self.each(8, lambda step: self.column_copy(step).wait_send())
        self.each(16, lambda step: self.gather_copy(step).wait_send())
        self.share_copy(self.core).wait_send()


def sum_scratch():
    return [
        pltpu.VMEM((HALF, 128), jnp.float32),
        pltpu.VMEM((HALF, 128), jnp.float32),
        pltpu.VMEM((16, PIECE, 128), jnp.float32),
        pltpu.VMEM((8, PIECE, 128), jnp.float32),
        pltpu.VMEM((2, 16, PIECE, 128), jnp.bfloat16),
        pltpu.SemaphoreType.DMA((2,)),
        pltpu.SemaphoreType.DMA((2, 16)),
        pltpu.SemaphoreType.DMA((2, 8)),
        pltpu.SemaphoreType.DMA((2, 16)),
        pltpu.SemaphoreType.DMA((2,)),
    ]


class Halo:
    def __init__(self, block, packed, rows, cols, corners, sems):
        self.block, self.packed, self.rows, self.cols, self.corners, self.sems = block, packed, rows, cols, corners, sems
        self.lon, self.lat = lax.axis_index("lon"), lax.axis_index("lat")

    def crosses(self, v):
        return self.lat == (0 if v < 0 else 7)

    def device(self, v, h):
        if v == 0:
            return {"lon": (self.lon + h + 32) % 32, "lat": self.lat}
        crosses = self.crosses(v)
        lon = (self.lon + h + 32 + jnp.where(crosses, 16, 0)) % 32
        return {"lon": lon, "lat": jnp.where(crosses, self.lat, self.lat + v)}

    def copy(self, v, h, receiving=False):
        first = 0 if v < 0 else PAIRS - 1
        side = 0 if h < 0 else 1
        if receiving:
            across, along = (0 if v < 0 else 1), side
            row, col = v + 1, h + 1
        else:
            crosses = self.crosses(v) if v else False
            across = jnp.where(crosses, 0 if v < 0 else 1, 1 if v < 0 else 0) if v else 0
            along = 1 - side
            row, col = (jnp.where(crosses, v + 1, 1 - v) if v else 1), 1 - h
        if h == 0:
            source, target = self.block.at[:, first], self.rows.at[across]
        elif v == 0:
            source, target = self.packed.at[side], self.cols.at[along]
        else:
            source, target = self.packed.at[side, :, first], self.corners.at[across, along]
        return pltpu.make_async_remote_copy(
            src_ref=source, dst_ref=target,
            send_sem=self.sems.at[0, v + 1, h + 1], recv_sem=self.sems.at[1, row, col],
            device_id=self.device(v, h), device_id_type=pl.DeviceIdType.MESH,
        )

    def pack(self):
        self.packed[0] = self.block[:, :, :, 0:2, :]
        self.packed[1] = self.block[:, :, :, COLS - 2 : COLS, :]

    def send(self):
        for v, h in SIDES:
            self.copy(v, h).start()

    def place(self, wide):
        wide[:, 2:34, 2:26, :] = self.block[...].reshape(2, 32, COLS, 128).astype(F32)
        for v, h in SIDES:
            self.copy(v, h, True).wait_recv()
        for side in range(2):
            wide[:, 2:34, pl.ds(26 * side, 2), :] = self.cols[side].reshape(2, 32, 2, 128).astype(F32)
        for across in range(2):
            crosses = self.crosses(-1 if across == 0 else 1)
            for row in range(2):
                target = 34 * across + jnp.where(crosses, 1 - row, row)
                wide[:, target, 2:26, :] = self.rows[across, :, row].astype(F32)
                for side in range(2):
                    wide[:, target, pl.ds(26 * side, 2), :] = self.corners[across, side, :, row].astype(F32)

    def close(self):
        for v, h in SIDES:
            self.copy(v, h).wait_send()


def halo_scratch():
    return [
        pltpu.VMEM((2, 2, PAIRS, 2, 2, 128), BF16),
        pltpu.VMEM((2, 2, 2, COLS, 128), BF16),
        pltpu.VMEM((2, 2, PAIRS, 2, 2, 128), BF16),
        pltpu.VMEM((2, 2, 2, 2, 2, 128), BF16),
        pltpu.SemaphoreType.DMA((2, 3, 3)),
    ]


def each_sample(act):
    def step(n, carry):
        act(n)
        return carry

    lax.fori_loop(0, 2, step, 0)


def lay_taps(wide, taps, rows):
    flat = wide.reshape(2, wide.shape[1] * 32, 128)

    def one(n):
        for b in range(3):
            shifted = flat[n, pl.ds(b, rows * 32), :].astype(BF16)
            taps[n, :, :, :, b * 128 : (b + 1) * 128] = shifted.reshape(rows // 2, 2, 32, 128)

    each_sample(one)


def pair_rows(taps, n, pairs):
    parts = [taps[n, q // 2 : q // 2 + pairs, q % 2].reshape(pairs * 32, WIDE) for q in range(4)]
    return jnp.concatenate(parts, axis=1)


def forward(taps, matrix, n, pairs):
    got = jnp.dot(pair_rows(taps, n, pairs), matrix[...], preferred_element_type=F32)
    return got.reshape(pairs, 32, 256)


def turned(left, right):
    return lax.dot_general(left, right, (((1,), (1,)), ((), ())), preferred_element_type=F32)


def backward(taps, matrix, n, pairs):
    return turned(pair_rows(taps, n, pairs), matrix[...]).reshape(pairs, 32, 256)


def lay_weights(weights, ahead, back):
    for q in range(4):
        for o in range(2):
            for b in range(3):
                tap, span = q - o, pl.ds(q * WIDE + b * 128, 128)
                inside = 0 <= tap <= 2
                lanes = pl.ds(o * 128, 128)
                ahead[span, lanes] = weights[tap * 3 + b] if inside else jnp.zeros((128, 128), BF16)
                back[lanes, span] = weights[(2 - tap) * 3 + 2 - b] if inside else jnp.zeros((128, 128), BF16)


def outer_sum(taps, grads, result, rows):
    total = None
    for n in range(2):
        part = lax.dot_general(
            taps[n].reshape(rows * 32, WIDE), grads[n].reshape(rows * 32, WIDE),
            (((0,), (0,)), ((), ())), preferred_element_type=F32,
        )
        total = part if total is None else total + part
    for a in range(3):
        for b in range(3):
            result[pl.ds((3 * a + b) * 128, 128)] = total[b * 128 : (b + 1) * 128, a * 128 : (a + 1) * 128]


def block_kernel(field, cotangent, w_one, w_two, output, field_grad, first_sum, second_sum, *scratch):
    (wide_f, wide_c, wide_h, wide_p, taps_f, taps_c, taps_h, taps_p, pre, grads_c, grads_p,
     ahead_one, back_one, ahead_two, back_two, first, second) = scratch[:17]
    halo_f = Halo(field, *scratch[17:22])
    halo_c = Halo(cotangent, *scratch[22:27])
    sum_two = Sum(second, second_sum, *scratch[27:32], scratch[32:37])
    sum_one = Sum(first, first_sum, *scratch[37:42], scratch[42:47])
    lat = lax.axis_index("lat")
    top = lat == 0
    at_pole = jnp.logical_or(top, lat == 7)

    barrier = pltpu.get_barrier_semaphore()

    def greet(device):
        pl.semaphore_signal(barrier, inc=1, device_id=device, device_id_type=pl.DeviceIdType.MESH)

    for v, h in SIDES:
        greet(halo_f.device(v, h))
    greet(sum_one.partner())
    sum_one.each(16, lambda step: greet(sum_one.plane_peer(step)[1]))
    sum_one.each(8, lambda step: greet(sum_one.column_peer(step)[1]))
    halo_f.pack()
    halo_c.pack()
    pl.semaphore_wait(barrier, 31)
    halo_f.send()
    halo_c.send()

    lay_weights(w_one, ahead_one, back_one)
    lay_weights(w_two, ahead_two, back_two)
    for wide in (wide_f, wide_c):
        wide[:, 0:36, 28:32, :] = jnp.zeros((2, 36, 4, 128), F32)
        wide[:, 36, :, :] = jnp.zeros((2, 32, 128), F32)
    for wide in (wide_h, wide_p):
        wide[:, 34, :, :] = jnp.zeros((2, 32, 128), F32)
    grads_c[...] = jnp.zeros(grads_c.shape, BF16)
    grads_p[...] = jnp.zeros(grads_p.shape, BF16)
    for a in range(3):
        grads_c[:, a : a + 32, 0:24, a * 128 : (a + 1) * 128] = cotangent[...].reshape(2, 32, COLS, 128)

    halo_f.place(wide_f)
    lay_taps(wide_f, taps_f, 36)

    def pre_one(n):
        got = forward(taps_f, ahead_one, n, 17)
        for o in range(2):
            pre[n, pl.ds(o, 17, stride=2)] = got[:, :, o * 128 : (o + 1) * 128]

    each_sample(pre_one)

    @pl.when(at_pole)
    def _():
        row = jnp.where(top, 0, 33)
        for n in range(2):
            got = None
            for q in range(3):
                right = w_one[pl.ds(3 * (2 - q), 3)].reshape(WIDE, 128)
                part = jnp.dot(taps_f[n, (row + q) // 2, (row + q) % 2], right, preferred_element_type=F32)
                got = part if got is None else got + part
            pre[n, row] = got

    def hidden_one(n):
        value = pre[n]
        wide_h[n, 0:34] = value / (1.0 + jnp.exp(-value))

    each_sample(hidden_one)
    lay_taps(wide_h, taps_h, 34)
    outer_sum(taps_h, grads_c, second, 34)
    sum_two.start()

    halo_c.place(wide_c)
    lay_taps(wide_c, taps_c, 36)

    def hidden_grad_one(n):
        got = backward(taps_c, back_two, n, 17)
        for o in range(2):
            wide_p[n, pl.ds(o, 17, stride=2)] = got[:, :, o * 128 : (o + 1) * 128]

    each_sample(hidden_grad_one)
    sign = jnp.where(top, 1.0, -1.0)

    @pl.when(at_pole)
    def _():
        row = jnp.where(top, 0, 32)
        source = jnp.where(top, 0, 17)
        for n in range(2):
            left = taps_c[n, source].reshape(64, WIDE)
            change = turned(left, back_two[0:128, 768:1152]) - turned(left, back_two[0:128, 0:384])
            wide_p[n, pl.ds(row, 2)] += (sign * change).reshape(2, 32, 128)

    def pre_grad_one(n):
        value = pre[n]
        s = 1.0 / (1.0 + jnp.exp(-value))
        grad = wide_p[n, 0:34] * s * (1.0 + value * (1.0 - s))
        wide_p[n, 0:34] = grad
        place = lax.broadcasted_iota(jnp.int32, (32, 32, 128), 1)
        inner = jnp.where(jnp.logical_and(place >= 1, place <= 24), grad[1:33], 0.0).astype(BF16)
        for a in range(3):
            grads_p[n, pl.ds(1 + a, 32), :, a * 128 : (a + 1) * 128] = inner

    each_sample(pre_grad_one)
    sum_two.to_plane()
    outer_sum(taps_f, grads_p, first, 36)
    sum_one.start()
    sum_two.to_column()

    def output_one(n):
        got = forward(taps_h, ahead_two, n, 16)
        for o in range(2):
            kept = got[:, 0:24, o * 128 : (o + 1) * 128]
            output[n, :, o] = (field[n, :, o].astype(F32) + kept).astype(BF16)

    each_sample(output_one)
    sum_one.to_plane()
    sum_two.to_gather()
    lay_taps(wide_p, taps_p, 34)

    def field_grad_one(n):
        got = backward(taps_p, back_one, n, 16)
        for o in range(2):
            wide_f[n, pl.ds(o, 16, stride=2)] = got[:, :, o * 128 : (o + 1) * 128]

    each_sample(field_grad_one)

    @pl.when(at_pole)
    def _():
        row = jnp.where(top, 0, 31)
        source = jnp.where(top, 0, 33)
        for n in range(2):
            left = taps_p[n, source // 2, source % 2]
            change = turned(left, back_one[0:128, 768:1152]) - turned(left, back_one[0:128, 0:384])
            wide_f[n, row] += sign * change

    sum_one.to_column()

    def keep_one(n):
        kept = wide_f[n, 0:32, 0:24].reshape(PAIRS, 2, COLS, 128)
        field_grad[n] = (cotangent[n].astype(F32) + kept).astype(BF16)

    each_sample(keep_one)
    sum_two.to_share()
    sum_one.to_gather()
    sum_two.finish()
    sum_one.to_share()
    sum_one.finish()
    halo_f.close()
    halo_c.close()


def body(field, cotangent, first_weights, second_weights):
    vmem = pl.BlockSpec(memory_space=pltpu.VMEM)
    grad = jax.ShapeDtypeStruct((2 * HALF, 128), BF16)
    cells = jax.ShapeDtypeStruct((2, PAIRS, 2, COLS, 128), BF16)
    matrix = [pltpu.VMEM((4 * WIDE, 256), BF16), pltpu.VMEM((256, 4 * WIDE), BF16)]
    output, field_grad, first, second = pl.pallas_call(
        block_kernel,
        out_shape=(cells, cells, grad, grad),
        in_specs=[vmem] * 4,
        out_specs=(vmem,) * 4,
        scratch_shapes=[
            pltpu.VMEM((2, 37, 32, 128), F32),
            pltpu.VMEM((2, 37, 32, 128), F32),
            pltpu.VMEM((2, 35, 32, 128), F32),
            pltpu.VMEM((2, 35, 32, 128), F32),
            pltpu.VMEM((2, 18, 2, 32, WIDE), BF16),
            pltpu.VMEM((2, 18, 2, 32, WIDE), BF16),
            pltpu.VMEM((2, 17, 2, 32, WIDE), BF16),
            pltpu.VMEM((2, 17, 2, 32, WIDE), BF16),
            pltpu.VMEM((2, 34, 32, 128), F32),
            pltpu.VMEM((2, 34, 32, WIDE), BF16),
            pltpu.VMEM((2, 36, 32, WIDE), BF16),
        ]
        + matrix
        + matrix
        + [pltpu.VMEM((2 * HALF, 128), F32)] * 2
        + halo_scratch()
        + halo_scratch()
        + sum_scratch()
        + sum_scratch(),
        compiler_params=pltpu.CompilerParams(
            collective_id=0, has_side_effects=True, vmem_limit_bytes=60 * 1024 * 1024
        ),
    )(field.reshape(cells.shape), cotangent.reshape(cells.shape), first_weights.reshape(9, 128, 128), second_weights.reshape(9, 128, 128))
    first, second = (one.astype(F32).reshape(3, 3, 128, 128) for one in (first, second))
    return output.reshape(field.shape), field_grad.reshape(field.shape), first, second


def solution(mesh):
    return jax.shard_map(
        body,
        mesh=mesh,
        in_specs=(P(None, "lat", "lon", None), P(None, "lat", "lon", None), P(), P()),
        out_specs=(P(None, "lat", "lon", None), P(None, "lat", "lon", None), P(), P()),
        check_vma=False,
    )
```

profile of v0, /device:TPU:1, one launch (start us, length us, event | category | flops | bytes accessed | tf_op | source)
XLA Modules:
  0.0 61.5 jit_solution(15735406861787009716)
XLA Ops:
  0.6 56.0 %shard_map.75 = (bf16[2,16,2,24,128]{4,3,2,1,0:T(8,128)(2,1)}, bf16[2,16,2,24,128]{4,3,2,1,0:T(8,128)(2,1)}, bf16[1152,128]{1,0:T(8,128)(2,1)}, bf16[1152,128]{1,0:T(8,128)(2,1)}) custom-call(bf16[2,16,2,24,128]{4,3,2,1,0:T(8,128)(2,1)} %bitcast.12, bf16[2,16,2,24,128]{4,3,2,1,0:T(8,128)(2,1)} %bitcast.13, bf16[9,128,128]{2,1,0:T(8,128)(2,1)} %bitcast.16, ...), custom_call_target="tpu_custom_call" | custom-call | tf_op jit(solution)/shard_map/pallas_call | solution.py:443
  56.7 0.0 copy-start.2
  56.7 1.9 %convert.2 = f32[3,3,128,128]{3,2,1,0:T(8,128)} convert(bf16[3,3,128,128]{3,2,1,0:T(8,128)(2,1)} %bitcast.15) | non-fusion elementwise | flops 147456 | bytes 884736 | tf_op jit(solution)/shard_map/reshape | solution.py:472
  58.5 0.0 copy-done.2
  58.5 0.0 copy-start.1
  58.5 0.9 %convert.3 = f32[3,3,128,128]{3,2,1,0:T(8,128)} convert(bf16[3,3,128,128]{3,2,1,0:T(8,128)(2,1)S(1)} %bitcast.14) | non-fusion elementwise | flops 147456 | bytes 884736 | tf_op jit(solution)/shard_map/reshape | solution.py:472
  59.4 0.2 copy-done.1
  59.7 0.0 copy-start
  59.7 0.7 %copy.10 = bf16[2,32,24,128]{3,2,1,0:T(8,128)(2,1)} copy(bf16[2,32,24,128]{3,2,1,0:T(8,128)(2,1)S(1)} %bitcast.11) | data formatting | bytes 786432
  60.4 0.4 copy-done
  60.8 0.7 %copy.11 = bf16[2,32,24,128]{3,2,1,0:T(8,128)(2,1)} copy(bf16[2,32,24,128]{3,2,1,0:T(8,128)(2,1)S(1)} %bitcast.10) | data formatting | bytes 786432
Async XLA Ops:
  56.7 1.9 %copy-start.2 = (bf16[1152,128]{1,0:T(8,128)(2,1)S(1)}, bf16[1152,128]{1,0:T(8,128)(2,1)}, u32[]{:S(2)}) copy-start(bf16[1152,128]{1,0:T(8,128)(2,1)} %get-tuple-element.11) | copy-start | bytes 884740
  58.5 1.1 %copy-start.1 = (bf16[2,16,2,24,128]{4,3,2,1,0:T(8,128)(2,1)S(1)}, bf16[2,16,2,24,128]{4,3,2,1,0:T(8,128)(2,1)}, u32[]{:S(2)}) copy-start(bf16[2,16,2,24,128]{4,3,2,1,0:T(8,128)(2,1)} %get-tuple-element.8) | copy-start | bytes 1179652
  59.7 1.1 %copy-start = (bf16[2,16,2,24,128]{4,3,2,1,0:T(8,128)(2,1)S(1)}, bf16[2,16,2,24,128]{4,3,2,1,0:T(8,128)(2,1)}, u32[]{:S(2)}) copy-start(bf16[2,16,2,24,128]{4,3,2,1,0:T(8,128)(2,1)} %get-tuple-element.9) | copy-start | bytes 1179652
where the time goes:
time: 61.8 us; the launch traced here: 61.5 us
  Pallas kernels  56 us (91%)
  other arithmetic  2.73 us (4%)
  local copies, waits for them, and re-layouts  2.14 us (3%)
  between operations  0.65 us (1%)
    pallas_call x1, Pallas kernels, body(): pl.pallas_call(block_kernel, out_shape=(cells, cells, grad, grad), in_spe...  56 us
    reshape x2, other arithmetic, body(): one.astype(F32).reshape(3, 3, 128, 128)  2.73 us
    unnamed x8, local copies, waits for them, and re-layouts  2.14 us

commit v1 on v0

--- a/solution.py
+++ b/solution.py
@@ -22,14 +22,10 @@
     return lon, lat, core, x_lo, depth
 
 
-def offset_of(piece):
-    return pl.multiple_of(((9 * piece) // 2) * 8, 8)
-
-
 class Sum:
-    def __init__(self, partial, final, half, pair, plane, column, gathered, sems):
-        self.partial, self.final = partial, final
-        self.half, self.pair, self.plane, self.column, self.gathered = half, pair, plane, column, gathered
+    def __init__(self, partial, gathered, half, pair, plane, column, sems):
+        self.partial, self.gathered = partial, gathered
+        self.half, self.pair, self.plane, self.column = half, pair, plane, column
         self.pair_sem, self.plane_sem, self.column_sem, self.gather_sem, self.share_sem = sems
         self.lon, self.lat, self.core, self.x_lo, self.depth = positions()
         self.member = self.x_lo * 8 + self.lat
@@ -61,7 +57,7 @@
         peer, device = self.plane_peer(step)
         slot = peer if receiving else self.member
         return self.remote(
-            self.half.at[pl.ds(offset_of(peer), PIECE)], self.plane.at[slot],
+            self.half.at[peer], self.plane.at[slot],
             self.plane_sem.at[0, peer], self.plane_sem.at[1, slot], device,
         )
 
@@ -99,15 +95,18 @@
     def to_plane(self):
         self.pair_copy().wait_recv()
         own = pl.multiple_of(self.core * HALF, 8)
-        self.half[...] = self.partial[pl.ds(own, HALF)] + self.pair[...]
+        for piece in range(16):
+            first = ((9 * piece) // 2) * 8
+            mine = self.partial[pl.ds(pl.multiple_of(own + first, 8), PIECE)]
+            self.half[piece] = (mine + self.pair[pl.ds(first, PIECE)]).astype(BF16)
         self.each(16, lambda step: self.plane_copy(step).start())
-        self.plane[self.member] = self.half[pl.ds(offset_of(self.member), PIECE)]
+        self.plane[self.member] = self.half[self.member]
 
     def to_column(self):
         self.each(16, lambda step: self.plane_copy(step, True).wait_recv())
-        total = self.plane[0]
+        total = self.plane[0].astype(F32)
         for member in range(1, 16):
-            total = total + self.plane[member]
+            total = total + self.plane[member].astype(F32)
         self.column[self.depth] = total
         self.each(8, lambda step: self.column_copy(step).start())
 
@@ -125,10 +124,6 @@
 
     def finish(self):
         self.share_copy(1 - self.core).wait_recv()
-        for half in range(2):
-            for piece in range(16):
-                first = half * HALF + ((9 * piece) // 2) * 8
-                self.final[pl.ds(first, PIECE)] = self.gathered[half, piece]
         self.pair_copy().wait_send()
         self.each(16, lambda step: self.plane_copy(step).wait_send())
         self.each(8, lambda step: self.column_copy(step).wait_send())
@@ -138,11 +133,10 @@
 
 def sum_scratch():
     return [
-        pltpu.VMEM((HALF, 128), jnp.float32),
-        pltpu.VMEM((HALF, 128), jnp.float32),
-        pltpu.VMEM((16, PIECE, 128), jnp.float32),
-        pltpu.VMEM((8, PIECE, 128), jnp.float32),
-        pltpu.VMEM((2, 16, PIECE, 128), jnp.bfloat16),
+        pltpu.VMEM((16, PIECE, 128), BF16),
+        pltpu.VMEM((HALF, 128), F32),
+        pltpu.VMEM((16, PIECE, 128), BF16),
+        pltpu.VMEM((8, PIECE, 128), F32),
         pltpu.SemaphoreType.DMA((2,)),
         pltpu.SemaphoreType.DMA((2, 16)),
         pltpu.SemaphoreType.DMA((2, 8)),
@@ -197,8 +191,12 @@
         for v, h in SIDES:
             self.copy(v, h).start()
 
+    def fill(self, wide):
+        wide[:, 2:34, 2:26, :] = self.block[...].reshape(2, 32, COLS, 128).astype(F32)
+        wide[:, 0:36, 28:32, :] = jnp.zeros((2, 36, 4, 128), F32)
+        wide[:, 36, :, :] = jnp.zeros((2, 32, 128), F32)
+
     def place(self, wide):
-        wide[:, 2:34, 2:26, :] = self.block[...].reshape(2, 32, COLS, 128).astype(F32)
         for v, h in SIDES:
             self.copy(v, h, True).wait_recv()
         for side in range(2):
@@ -292,8 +290,8 @@
      ahead_one, back_one, ahead_two, back_two, first, second) = scratch[:17]
     halo_f = Halo(field, *scratch[17:22])
     halo_c = Halo(cotangent, *scratch[22:27])
-    sum_two = Sum(second, second_sum, *scratch[27:32], scratch[32:37])
-    sum_one = Sum(first, first_sum, *scratch[37:42], scratch[42:47])
+    sum_two = Sum(second, second_sum, *scratch[27:31], scratch[31:36])
+    sum_one = Sum(first, first_sum, *scratch[36:40], scratch[40:45])
     lat = lax.axis_index("lat")
     top = lat == 0
     at_pole = jnp.logical_or(top, lat == 7)
@@ -310,15 +308,10 @@
     sum_one.each(8, lambda step: greet(sum_one.column_peer(step)[1]))
     halo_f.pack()
     halo_c.pack()
-    pl.semaphore_wait(barrier, 31)
-    halo_f.send()
-    halo_c.send()
-
     lay_weights(w_one, ahead_one, back_one)
     lay_weights(w_two, ahead_two, back_two)
-    for wide in (wide_f, wide_c):
-        wide[:, 0:36, 28:32, :] = jnp.zeros((2, 36, 4, 128), F32)
-        wide[:, 36, :, :] = jnp.zeros((2, 32, 128), F32)
+    halo_f.fill(wide_f)
+    halo_c.fill(wide_c)
     for wide in (wide_h, wide_p):
         wide[:, 34, :, :] = jnp.zeros((2, 32, 128), F32)
     grads_c[...] = jnp.zeros(grads_c.shape, BF16)
@@ -326,6 +319,9 @@
     for a in range(3):
         grads_c[:, a : a + 32, 0:24, a * 128 : (a + 1) * 128] = cotangent[...].reshape(2, 32, COLS, 128)
 
+    pl.semaphore_wait(barrier, 31)
+    halo_f.send()
+    halo_c.send()
     halo_f.place(wide_f)
     lay_taps(wide_f, taps_f, 36)
 
@@ -435,12 +431,32 @@
     halo_c.close()
 
 
+def result_kernel(output, field_grad, first, second, output_out, field_grad_out, first_out, second_out, wide_one, wide_two, sems):
+    copies = [
+        pltpu.make_async_copy(output, output_out, sems.at[0]),
+        pltpu.make_async_copy(field_grad, field_grad_out, sems.at[1]),
+        pltpu.make_async_copy(wide_one, first_out, sems.at[2]),
+        pltpu.make_async_copy(wide_two, second_out, sems.at[3]),
+    ]
+    copies[0].start()
+    copies[1].start()
+    for source, target, copy in ((first, wide_one, copies[2]), (second, wide_two, copies[3])):
+        for half in range(2):
+            for piece in range(16):
+                row = half * HALF + ((9 * piece) // 2) * 8
+                target[pl.ds(row, PIECE)] = source[half, piece].astype(F32)
+        copy.start()
+    for copy in copies:
+        copy.wait()
+
+
 def body(field, cotangent, first_weights, second_weights):
     vmem = pl.BlockSpec(memory_space=pltpu.VMEM)
-    grad = jax.ShapeDtypeStruct((2 * HALF, 128), BF16)
+    grad = jax.ShapeDtypeStruct((2, 16, PIECE, 128), BF16)
+    whole = jax.ShapeDtypeStruct((2 * HALF, 128), F32)
     cells = jax.ShapeDtypeStruct((2, PAIRS, 2, COLS, 128), BF16)
     matrix = [pltpu.VMEM((4 * WIDE, 256), BF16), pltpu.VMEM((256, 4 * WIDE), BF16)]
-    output, field_grad, first, second = pl.pallas_call(
+    results = pl.pallas_call(
         block_kernel,
         out_shape=(cells, cells, grad, grad),
         in_specs=[vmem] * 4,
@@ -466,10 +482,18 @@
         + sum_scratch()
         + sum_scratch(),
         compiler_params=pltpu.CompilerParams(
-            collective_id=0, has_side_effects=True, vmem_limit_bytes=60 * 1024 * 1024
+            collective_id=0, has_side_effects=True, vmem_limit_bytes=32 * 1024 * 1024
         ),
     )(field.reshape(cells.shape), cotangent.reshape(cells.shape), first_weights.reshape(9, 128, 128), second_weights.reshape(9, 128, 128))
-    first, second = (one.astype(F32).reshape(3, 3, 128, 128) for one in (first, second))
+    output, field_grad, first, second = pl.pallas_call(
+        result_kernel,
+        out_shape=(cells, cells, whole, whole),
+        in_specs=[vmem] * 4,
+        out_specs=(pl.BlockSpec(memory_space=pl.ANY),) * 4,
+        scratch_shapes=[pltpu.VMEM((2 * HALF, 128), F32)] * 2 + [pltpu.SemaphoreType.DMA((4,))],
+        compiler_params=pltpu.CompilerParams(vmem_limit_bytes=8 * 1024 * 1024),
+    )(*results)
+    first, second = first.reshape(3, 3, 128, 128), second.reshape(3, 3, 128, 128)
     return output.reshape(field.shape), field_grad.reshape(field.shape), first, second
 
 

time: 61.8 us -> 57.3 us (0.927)
  Pallas kernels: 56 us -> 52.5 us
  other arithmetic: 2.73 us -> 0 us
  local copies, waits for them, and re-layouts: 2.14 us -> 3.91 us
    pallas_call x1, Pallas kernels: 56 us -> 51.2 us  [body(): pl.pallas_call(block_kernel, out_shape=(cells, cells, grad, grad), in_spe...]
    reshape x2 -> x0, other arithmetic: 2.73 us -> none  [body(): one.astype(F32).reshape(3, 3, 128, 128)]
    unnamed x8, local copies, waits for them, and re-layouts: 2.14 us -> 3.91 us
    pallas_call x0 -> x1, Pallas kernels: none -> 1.31 us  [body(): pl.pallas_call(result_kernel, out_shape=(cells, cells, whole, whole), in_...]
where the time goes in v1:
time: 57.3 us; the launch traced here: 57.1 us
  Pallas kernels  52.5 us (92%)
  local copies, waits for them, and re-layouts  3.91 us (7%)
  between operations  0.65 us (1%)
    pallas_call x1, Pallas kernels, body(): pl.pallas_call(block_kernel, out_shape=(cells, cells, grad, grad), in_spe...  51.2 us
    unnamed x8, local copies, waits for them, and re-layouts  3.91 us
    pallas_call x1, Pallas kernels, body(): pl.pallas_call(result_kernel, out_shape=(cells, cells, whole, whole), in_...  1.31 us

profile of v1, /device:TPU:1, one launch (start us, length us, event | category | flops | bytes accessed | tf_op | source)
XLA Modules:
  0.0 57.1 jit_solution(13958635551023118755)
XLA Ops:
  0.6 0.0 copy-start
  0.6 1.0 %copy-done = bf16[2,32,24,128]{3,2,1,0:T(8,128)(2,1)S(1)} copy-done((bf16[2,32,24,128]{3,2,1,0:T(8,128)(2,1)S(1)}, bf16[2,32,24,128]{3,2,1,0:T(8,128)(2,1)}, u32[]{:S(2)}) %copy-start) | copy-done | bytes 393240
  1.6 0.0 copy-start.1
  1.6 1.0 %copy-done.1 = bf16[2,32,24,128]{3,2,1,0:T(8,128)(2,1)S(1)} copy-done((bf16[2,32,24,128]{3,2,1,0:T(8,128)(2,1)S(1)}, bf16[2,32,24,128]{3,2,1,0:T(8,128)(2,1)}, u32[]{:S(2)}) %copy-start.1) | copy-done | bytes 393240
  2.6 0.0 copy-start.2
  2.6 1.0 %copy-done.2 = bf16[3,3,128,128]{3,2,1,0:T(8,128)(2,1)S(1)} copy-done((bf16[3,3,128,128]{3,2,1,0:T(8,128)(2,1)S(1)}, bf16[3,3,128,128]{3,2,1,0:T(8,128)(2,1)}, u32[]{:S(2)}) %copy-start.2) | copy-done | bytes 294936
  3.6 0.0 copy-start.3
  3.6 1.0 %copy-done.3 = bf16[3,3,128,128]{3,2,1,0:T(8,128)(2,1)S(1)} copy-done((bf16[3,3,128,128]{3,2,1,0:T(8,128)(2,1)S(1)}, bf16[3,3,128,128]{3,2,1,0:T(8,128)(2,1)}, u32[]{:S(2)}) %copy-start.3) | copy-done | bytes 294936
  4.5 51.2 %shard_map.75 = (bf16[2,16,2,24,128]{4,3,2,1,0:T(8,128)(2,1)S(1)}, bf16[2,16,2,24,128]{4,3,2,1,0:T(8,128)(2,1)S(1)}, bf16[2,16,40,128]{3,2,1,0:T(8,128)(2,1)S(1)}, bf16[2,16,40,128]{3,2,1,0:T(8,128)(2,1)S(1)}) custom-call(bf16[2,16,2,24,128]{4,3,2,1,0:T(8,128)(2,1)S(1)} %bitcast.8, bf16[2,16,2,24,128]{4,3,2,1,0:T(8,128)(2,1)S(1)} %bitcast.9, ...), custom_call_target="tpu_custom_call" | custom-call | tf_op jit(solution)/shard_map/pallas_call | solution.py:459
  55.8 1.3 %shard_map.76 = (bf16[2,16,2,24,128]{4,3,2,1,0:T(8,128)(2,1)}, bf16[2,16,2,24,128]{4,3,2,1,0:T(8,128)(2,1)}, f32[1152,128]{1,0:T(8,128)}, f32[1152,128]{1,0:T(8,128)}) custom-call(bf16[2,16,2,24,128]{4,3,2,1,0:T(8,128)(2,1)S(1)} %get-tuple-element.12.output, bf16[2,16,2,24,128]{4,3,2,1,0:T(8,128)(2,1)S(1)} %get-tuple-element.13.field_grad, ...), custom_call_target="tpu_custom_call" | custom-call | tf_op jit(solution)/shard_map/pallas_call | solution.py:488
Async XLA Ops:
  0.6 1.0 %copy-start = (bf16[2,32,24,128]{3,2,1,0:T(8,128)(2,1)S(1)}, bf16[2,32,24,128]{3,2,1,0:T(8,128)(2,1)}, u32[]{:S(2)}) copy-start(bf16[2,32,24,128]{3,2,1,0:T(8,128)(2,1)} %param.4) | copy-start | bytes 1179652
  1.6 1.0 %copy-start.1 = (bf16[2,32,24,128]{3,2,1,0:T(8,128)(2,1)S(1)}, bf16[2,32,24,128]{3,2,1,0:T(8,128)(2,1)}, u32[]{:S(2)}) copy-start(bf16[2,32,24,128]{3,2,1,0:T(8,128)(2,1)} %param.5) | copy-start | bytes 1179652
  2.6 1.0 %copy-start.2 = (bf16[3,3,128,128]{3,2,1,0:T(8,128)(2,1)S(1)}, bf16[3,3,128,128]{3,2,1,0:T(8,128)(2,1)}, u32[]{:S(2)}) copy-start(bf16[3,3,128,128]{3,2,1,0:T(8,128)(2,1)} %param.6) | copy-start | bytes 884740
  3.6 1.0 %copy-start.3 = (bf16[3,3,128,128]{3,2,1,0:T(8,128)(2,1)S(1)}, bf16[3,3,128,128]{3,2,1,0:T(8,128)(2,1)}, u32[]{:S(2)}) copy-start(bf16[3,3,128,128]{3,2,1,0:T(8,128)(2,1)} %param.7) | copy-start | bytes 884740
